TPU v7x, 32 devices: a whole 2x2x4 slice. The times are simulated.
32 devices in a mesh: lon: 4 (over x, core), frame: 8 (over z, y).
Axes of the slice: x: 2, y: 2, z: 4, core: 2. Of those that a mesh axis runs over, the one named last changes fastest.
Arguments:
- layer_input: bfloat16 [8, 16, 512, 128], P('frame', None, 'lon'), may hold values from -6 to 6
- hidden_saved: bfloat16 [8, 16, 512, 128], P('frame', None, 'lon'), as said below
- conv_weight: bfloat16 [3, 3, 128, 128], replicated, may hold values from -0.1875 to 0.1875
- queries: bfloat16 [2048, 128], P('lon'), may hold values from -6 to 6
- corr_cotangent: bfloat16 [8, 49, 2048], P('frame', None, 'lon'), may hold values from -0.59765625 to 0.59765625
- window_rows: int32 [8, 2048], P('frame', 'lon'), may hold values from 0 to 9
- window_cols: int32 [8, 2048], P('frame', 'lon'), may hold values from -3 to 124
- owner_strip: int32 [8, 2048, 1], P('frame', 'lon'), may hold values from 0 to 3; in each aligned block of 512 rows (0 to 511, 512 to 1023, ..., all dimensions but the last counted through in order) at most 128 rows name the same one
Outputs:
- query_grad: float32 [2048, 128], P(('lon', 'frame'))
- first_weight_grad: float32 [3, 3, 128, 128], replicated
- second_weight_grad: float32 [3, 3, 128, 128], replicated
Inputs may be any that keep to these rules, and one draw needn't show every extreme that they name: `hidden_saved`: rectifier outputs: zero or positive, a third or more of them exactly zero. `owner_strip`: in each frame, at most 128 of the 512 tracks homed on one strip name the same owning strip.
All inputs are finite; a program needn't handle non-finite values.
Results may differ from a plain program's by a relative error of at most 0.0045.
Values may be sent and summed in bfloat16 or wider, within the bound.
A program may use at most 64 MiB of HBM per device.

v0:
```python
import math

import jax
import jax.numpy as jnp
from jax import lax
from jax.sharding import PartitionSpec as P

WIN = 7


def padded_2(value, sides, width):
    for axis, dim in sides:
        peers, length = (lax.axis_size(axis), value.shape[dim])
        up = [(i, (i + 1) % peers) for i in range(peers)]
        down = [(j, i) for i, j in up]
        last = lax.slice_in_dim(value, length - width, length, axis=dim)
        first = lax.slice_in_dim(value, 0, width, axis=dim)
        before = lax.ppermute(last, axis, up)
        after = lax.ppermute(first, axis, down)
        value = jnp.concatenate([before, value, after], axis=dim)
    return value


def from_behind(value, axis, steps):
    count = lax.axis_size(axis)
    pairs = [(source, (source + steps) % count) for source in range(count)]
    return lax.ppermute(value, axis, pairs)


def pad_rows(field):
    return jnp.pad(field, ((1, 1), (0, 0), (0, 0)))


def conv_cells(padded, weight, out_cols):
    row_count = padded.shape[0] - 2
    result = jnp.zeros((row_count, out_cols, weight.shape[3]), jnp.float32)
    for row_tap in range(3):
        for col_tap in range(3):
            window = padded[row_tap : row_tap + row_count, col_tap : col_tap + out_cols]
            result = result + jnp.einsum(
                "rci,io->rco", window, weight[row_tap, col_tap], preferred_element_type=jnp.float32
            )
    return result


def conv_back(padded, weight, out_cols):
    row_count = padded.shape[0] - 2
    result = jnp.zeros((row_count, out_cols, weight.shape[2]), jnp.float32)
    for row_tap in range(3):
        for col_tap in range(3):
            window = padded[
                2 - row_tap : 2 - row_tap + row_count, 2 - col_tap : 2 - col_tap + out_cols
            ]
            result = result + jnp.einsum(
                "rco,io->rci", window, weight[row_tap, col_tap], preferred_element_type=jnp.float32
            )
    return result


def weight_terms(padded, grad):
    row_count, col_count, out_channels = grad.shape
    flat_grad = grad.reshape(row_count * col_count, out_channels)
    tap_terms = []
    for row_tap in range(3):
        for col_tap in range(3):
            window = padded[row_tap : row_tap + row_count, col_tap : col_tap + col_count].reshape(
                row_count * col_count, padded.shape[2]
            )
            tap_terms.append(
                lax.dot_general(
                    window, flat_grad, (((0,), (0,)), ((), ())), preferred_element_type=jnp.float32
                )
            )
    return jnp.stack(tap_terms).reshape(3, 3, padded.shape[2], out_channels)


def per_device(
    layer_input,
    hidden_saved,
    conv_weight,
    queries,
    corr_cotangent,
    window_rows,
    window_cols,
    owner_strip,
):
    strip_count = lax.axis_size("lon")
    input_local = layer_input[0]
    hidden_local = hidden_saved[0]
    row_count, col_count, channels = hidden_local.shape
    track_count = queries.shape[0]
    capacity = track_count // 4
    slot_count = strip_count * capacity
    wide_cols = col_count + 6
    taps_total = WIN * WIN
    reach = 4
    stacked = jnp.stack([input_local, hidden_local])
    edged = padded_2(stacked, (("lon", 2),), reach)
    input_edged = pad_rows(edged[0, :, reach - 1 : reach + col_count + 1])
    hidden_edged = pad_rows(edged[1, :, reach - 1 : reach + col_count + 1])
    feature_wide = conv_cells(pad_rows(edged[1]), conv_weight, wide_cols).astype(jnp.bfloat16)
    owners = owner_strip[0, :, 0]
    strip_ids = jnp.arange(strip_count, dtype=jnp.int32)
    marks = (owners[:, None] == strip_ids[None, :]).astype(jnp.int32)
    before = jnp.cumsum(marks, axis=0) - marks
    position = jnp.sum(before * marks, axis=1)
    slot_index = owners * capacity + position
    cot_rows = jnp.pad(corr_cotangent[0].T, ((0, 0), (0, 128 - taps_total)))
    meta_home = jnp.stack([window_rows[0], window_cols[0] + 3], axis=1)
    payload = jnp.concatenate([queries, cot_rows], axis=1)
    send_payload = (
        jnp.zeros((slot_count, payload.shape[1]), jnp.bfloat16).at[slot_index].set(payload)
    )
    send_meta = jnp.zeros((slot_count, meta_home.shape[1]), jnp.int32).at[slot_index].set(meta_home)
    got_payload, got_meta = (
        lax.all_to_all(send_payload, "lon", split_axis=0, concat_axis=0, tiled=True),
        lax.all_to_all(send_meta, "lon", split_axis=0, concat_axis=0, tiled=True),
    )
    query_slots = got_payload[:, :channels]
    cot_slots = got_payload[:, channels : channels + taps_total]
    block_rows = math.gcd(slot_count, 512)
    block_count = slot_count // block_rows
    feature_flat = feature_wide.reshape(row_count * wide_cols, channels)
    offsets = jnp.arange(WIN, dtype=jnp.int32)
    row_ids = jnp.arange(row_count, dtype=jnp.int32)
    col_ids = jnp.arange(wide_cols, dtype=jnp.int32)

    def block_step(grad_acc, block_items):
        cot_block, meta_block, query_block = block_items
        cot_square = cot_block.reshape(block_rows, WIN, WIN)
        row_hot = (
            meta_block[:, 0][:, None, None] + offsets[None, :, None] == row_ids[None, None, :]
        ).astype(jnp.bfloat16)
        col_hot = (
            meta_block[:, 1][:, None, None] + offsets[None, :, None] == col_ids[None, None, :]
        ).astype(jnp.bfloat16)
        placed_cols = jnp.einsum(
            "tij,tjh->tih", cot_square, col_hot, preferred_element_type=jnp.float32
        ).astype(jnp.bfloat16)
        spread = jnp.einsum(
            "tir,tih->trh", row_hot, placed_cols, preferred_element_type=jnp.float32
        ).astype(jnp.bfloat16)
        spread = spread.reshape(block_rows, row_count * wide_cols)
        block_grads = jnp.dot(spread, feature_flat, preferred_element_type=jnp.float32)
        grad_acc = grad_acc + lax.dot_general(
            spread, query_block, (((0,), (0,)), ((), ())), preferred_element_type=jnp.float32
        )
        return (grad_acc, block_grads)

    block_items = (
        cot_slots.reshape(block_count, block_rows, taps_total),
        got_meta.reshape(block_count, block_rows, got_meta.shape[1]),
        query_slots.reshape(block_count, block_rows, channels),
    )
    grad_flat, query_blocks = lax.scan(
        block_step, jnp.zeros((row_count * wide_cols, channels), jnp.float32), block_items
    )
    slot_grads = query_blocks.reshape(slot_count, channels)
    returned = lax.all_to_all(slot_grads, "lon", split_axis=0, concat_axis=0, tiled=True)
    home_grads = returned[slot_index]
    query_grad = lax.psum_scatter(home_grads, "frame", scatter_dimension=0, tiled=True)
    grad_wide = grad_flat.reshape(row_count, wide_cols, channels)
    from_prior = from_behind(grad_wide[:, col_count + 3 :], "lon", 1)
    from_next = from_behind(grad_wide[:, :3], "lon", -1)
    own_grad = grad_wide[:, 3 : col_count + 3]
    own_grad = own_grad.at[:, :3].add(from_prior)
    own_grad = own_grad.at[:, col_count - 3 :].add(from_next)
    grad_edged = padded_2(own_grad.astype(jnp.bfloat16), (("lon", 1),), 1)
    feature_grad = grad_edged[:, 1 : col_count + 1]
    hidden_grad = conv_back(pad_rows(grad_edged), conv_weight, col_count)
    pre_grad = jnp.where(hidden_local > 0, hidden_grad, jnp.zeros_like(hidden_grad)).astype(
        jnp.bfloat16
    )
    second_term = weight_terms(hidden_edged, feature_grad)
    first_term = weight_terms(input_edged, pre_grad)
    first_sum, second_sum = lax.psum((first_term, second_term), ("lon", "frame"))
    norm_factor = 1.0 / math.sqrt(row_count * col_count * strip_count * lax.axis_size("frame"))
    return (query_grad, first_sum * norm_factor, second_sum * norm_factor)


def solution(mesh):
    placed = (
        P("frame", None, "lon", None),
        P("frame", None, "lon", None),
        P(),
        P("lon", None),
        P("frame", None, "lon"),
        P("frame", "lon"),
        P("frame", "lon"),
        P("frame", "lon", None),
    )
    return jax.shard_map(
        per_device,
        mesh=mesh,
        in_specs=placed,
        out_specs=(P(("lon", "frame"), None), P(), P()),
        check_vma=False,
    )
```

profile of v0, /device:TPU:0, one launch (start us, length us, event | category | flops | bytes accessed | tf_op | source)
XLA Modules:
  0.0 221.2 jit_solution(16327299058159711779)
XLA Ops:
  8.8 1.2 reduce-window.6
  13.4 1.8 scatter_custom_fusion
  15.9 4.2 %all-to-all-start = ((s32[4,128,2]{1,2,0:T(2,128)}), s32[4,128,2]{1,2,0:T(2,128)S(1)}, u32[]{:S(2)}, u32[]{:S(2)}) async-start(s32[4,128,2]{1,2,0:T(2,128)} %copy.76), calls=%async_computation | async-start | bytes 8192 | tf_op jit(solution)/shard_map/all_to_all | solution.py:117
  20.3 1.8 collective-permute-start.1
  22.4 3.0 %scatter_custom_fusion.1 = bf16[512,256]{1,0:T(8,128)(2,1)} fusion(s32[512]{0:T(512)S(1)} %bitcast.248, bf16[512,256]{1,0:T(8,128)(2,1)S(1)} %copy.78, bf16[]{:T(256)} %constant.86.clone.1), kind=kCustom, calls=%fused_computation.147 | custom fusion | bytes 262146 | tf_op jit(solution)/shard_map/scatter | solution.py:112
  25.4 3.4 %all-to-all-start.1 = ((bf16[4,128,256]{2,1,0:T(8,128)(2,1)}), bf16[4,128,256]{2,1,0:T(8,128)(2,1)S(1)}, u32[]{:S(2)}, u32[]{:S(2)}) async-start(bf16[4,128,256]{2,1,0:T(8,128)(2,1)} %bitcast.13), calls=%async_computation.1 | async-start | bytes 524288 | tf_op jit(solution)/shard_map/all_to_all | solution.py:116
  29.9 0.9 copy-done.3
  34.2 1.3 fusion.9
  36.1 5.9 %fusion.1 = bf16[512,16,134]{2,1,0:T(8,128)(2,1)} fusion(bf16[512,7,7]{2,1,0:T(8,128)(2,1)S(1)} %reshape.292, s32[512,7]{1,0:T(8,128)S(1)} %get-tuple-element.69, s32[512,7]{1,0:T(8,128)S(1)} %get-tuple-element.70), kind=kOutput, calls=%fused_computation.5 | convolution fusion | flops 23109632 | bytes 2274304 | tf_op jit(solution)/shard_map/while/body/eval_jaxpr/tir,tih->trh/dot_general | solution.py:140
  42.0 7.9 %copy.81 = bf16[512,16,134]{0,1,2:T(8,128)(2,1)} copy(bf16[512,16,134]{2,1,0:T(8,128)(2,1)} %fusion.1) | data formatting | bytes 4390912 | tf_op jit(solution)/shard_map/while/body/eval_jaxpr/tir,tih->trh/dot_general | solution.py:140
  49.9 2.8 %copy.83 = bf16[512,16,134]{0,2,1:T(8,128)(2,1)S(1)} copy(bf16[512,16,134]{0,1,2:T(8,128)(2,1)} %copy.81) | data formatting | bytes 4390912 | tf_op jit(solution)/shard_map/while/body/eval_jaxpr/convert_element_type | solution.py:142
  52.7 2.1 reshape.236
  54.9 2.6 %dot_general.141 = bf16[16,134,512]{2,1,0:T(8,128)(2,1)S(1)} reshape(bf16[2144,512]{1,0:T(8,128)(2,1)} %bitcast.235) | data formatting | bytes 4390912 | tf_op jit(solution)/shard_map/while/body/eval_jaxpr/dot_general | solution.py:145
  57.5 1.6 fusion.97
  60.2 1.3 collective-permute-start.3
  61.5 1.1 collective-permute-done.2
  63.7 1.8 collective-permute-start.5
  77.5 2.5 %fusion.46 = f32[512,128,1]{1,0,2:T(8,128)} fusion(bf16[512,16,134]{0,1,2:T(8,128)(2,1)S(1)} %copy-done, bf16[16,134,128]{2,1,0:T(8,128)(2,1)} %fusion.9), kind=kOutput, calls=%fused_computation.87 | convolution fusion | flops 281018368 | bytes 3006464 | tf_op jit(solution)/shard_map/while/body/eval_jaxpr/dot_general | solution.py:144
  80.0 3.4 %all-to-all-start.2 = ((f32[4,128,128]{2,1,0:T(8,128)}), f32[4,128,128]{2,1,0:T(8,128)S(1)}, u32[]{:S(2)}, u32[]{:S(2)}) async-start(f32[4,128,128]{2,1,0:T(8,128)} %bitcast.36), calls=%async_computation.2 | async-start | bytes 524288 | tf_op jit(solution)/shard_map/all_to_all | solution.py:159
  83.5 6.6 %all-to-all-done.2 = f32[4,128,128]{2,1,0:T(8,128)S(1)} async-done(((f32[4,128,128]{2,1,0:T(8,128)}), f32[4,128,128]{2,1,0:T(8,128)S(1)}, u32[]{:S(2)}, u32[]{:S(2)}) %all-to-all-start.2) | async-done | bytes 262176 | tf_op jit(solution)/shard_map/all_to_all | solution.py:159
  90.1 1.6 gather_fusion
  91.8 119.1 %all-reduce.8.cloned.1.call-done = (f32[3,3,128,128]{3,2,1,0:T(8,128)}, f32[3,3,128,128]{3,2,1,0:T(8,128)}) async-done(((f32[3,3,128,128]{3,2,1,0:T(8,128)}, f32[3,3,128,128]{3,2,1,0:T(8,128)}), (f32[3,3,128,128]{3,2,1,0:T(8,128)}, f32[3,3,128,128]{3,2,1,0:T(8,128)})) %all-reduce.8.cloned.1.call-update) | async-done | bytes 1179664 | tf_op jit(solution)/shard_map/psum | solution.py:176
  210.9 2.0 broadcast_multiply_fusion.1
  212.9 0.9 broadcast_multiply_fusion
  (106 shorter events, 24.3 us)
Async XLA Ops:
  8.0 12.1 %copy-start.9 = (bf16[1,16,128,128]{3,2,1,0:T(8,128)(2,1)S(1)}, bf16[1,16,128,128]{3,2,1,0:T(8,128)(2,1)}, u32[]{:S(2)}) copy-start(bf16[1,16,128,128]{3,2,1,0:T(8,128)(2,1)} %param.12) | copy-start | bytes 1572868
  8.0 12.2 %copy-start.1 = (bf16[1,16,128,128]{3,2,1,0:T(8,128)(2,1)S(1)}, bf16[1,16,128,128]{3,2,1,0:T(8,128)(2,1)}, u32[]{:S(2)}) copy-start(bf16[1,16,128,128]{3,2,1,0:T(8,128)(2,1)} %param.13) | copy-start | bytes 1572868
  15.9 9.5 %all-to-all-start = ((s32[4,128,2]{1,2,0:T(2,128)}), s32[4,128,2]{1,2,0:T(2,128)S(1)}, u32[]{:S(2)}, u32[]{:S(2)}) async-start(s32[4,128,2]{1,2,0:T(2,128)} %copy.76), calls=%async_computation | async-start | bytes 8192 | tf_op jit(solution)/shard_map/all_to_all | solution.py:117
  20.1 2.0 copy-start.10
  20.1 2.1 copy-start.11
  20.3 9.0 %collective-permute-start.1 = (bf16[2,16,4,128]{3,2,1,0:T(4,128)(2,1)S(1)}, bf16[2,16,4,128]{3,2,1,0:T(4,128)(2,1)S(1)}, u32[]{:S(2)}, u32[]{:S(2)}) collective-permute-start(bf16[2,16,4,128]{3,2,1,0:T(4,128)(2,1)S(1)} %get-tuple-element.64), channel_id=1, source_target_pairs={{8,0},{16,8},{24,16},{0,24},{9,1},{17,9},{25,17},{1,25},{10,2},{18... | collective-permute-start | bytes 98312 | tf_op jit(solution)/shard_map/ppermute | solution.py:19
  22.1 7.2 %collective-permute-start = (bf16[2,16,4,128]{3,2,1,0:T(4,128)(2,1)S(1)}, bf16[2,16,4,128]{3,2,1,0:T(4,128)(2,1)S(1)}, u32[]{:S(2)}, u32[]{:S(2)}) collective-permute-start(bf16[2,16,4,128]{3,2,1,0:T(4,128)(2,1)S(1)} %get-tuple-element.63), channel_id=1, source_target_pairs={{0,8},{8,16},{16,24},{24,0},{1,9},{9,17},{17,25},{25,1},{2,10},{10... | collective-permute-start | bytes 98312 | tf_op jit(solution)/shard_map/ppermute | solution.py:18
  25.4 10.1 %all-to-all-start.1 = ((bf16[4,128,256]{2,1,0:T(8,128)(2,1)}), bf16[4,128,256]{2,1,0:T(8,128)(2,1)S(1)}, u32[]{:S(2)}, u32[]{:S(2)}) async-start(bf16[4,128,256]{2,1,0:T(8,128)(2,1)} %bitcast.13), calls=%async_computation.1 | async-start | bytes 524288 | tf_op jit(solution)/shard_map/all_to_all | solution.py:116
  28.8 182.1 %all-reduce.8.cloned.1.call-start = ((), (), s32[]{:S(2)}) async-start(), calls=%async_computation.5 | async-start | bytes 2359296 | tf_op jit(solution)/shard_map/psum | solution.py:176
  29.8 1.0 copy-start.3
  35.5 6.5 %copy-start.5 = (bf16[4,128,256]{2,1,0:T(8,128)(2,1)}, bf16[4,128,256]{2,1,0:T(8,128)(2,1)S(1)}, u32[]{:S(2)}) copy-start(bf16[4,128,256]{2,1,0:T(8,128)(2,1)S(1)} %all-to-all-done.1) | copy-start | bytes 786436
  59.2 3.4 %collective-permute-start.2 = (f32[16,3,128]{2,1,0:T(4,128)S(1)}, f32[16,3,128]{2,1,0:T(4,128)S(1)}, u32[]{:S(2)}, u32[]{:S(2)}) collective-permute-start(f32[16,3,128]{2,1,0:T(4,128)S(1)} %get-tuple-element.62), channel_id=1, source_target_pairs={{0,8},{8,16},{16,24},{24,0},{1,9},{9,17},{17,25},{25,1},{2,10},{10... | collective-permute-start | bytes 73736 | tf_op jit(solution)/shard_map/ppermute | solution.py:27
  60.2 3.2 %copy-start.4 = (bf16[3,3,128,128]{3,2,1,0:T(8,128)(2,1)S(1)}, bf16[3,3,128,128]{3,2,1,0:T(8,128)(2,1)}, u32[]{:S(2)}) copy-start(bf16[3,3,128,128]{3,2,1,0:T(8,128)(2,1)} %param.14) | copy-start | bytes 884740
  60.2 2.9 %collective-permute-start.3 = (f32[16,3,128]{2,1,0:T(4,128)S(1)}, f32[16,3,128]{2,1,0:T(4,128)S(1)}, u32[]{:S(2)}, u32[]{:S(2)}) collective-permute-start(f32[16,3,128]{2,1,0:T(4,128)S(1)} %get-tuple-element.61), channel_id=1, source_target_pairs={{0,24},{8,0},{16,8},{24,16},{1,25},{9,1},{17,9},{25,17},{2,26},{10... | collective-permute-start | bytes 73736 | tf_op jit(solution)/shard_map/ppermute | solution.py:27
  63.7 5.4 %collective-permute-start.5 = (bf16[16,1,128]{2,1,0:T(2,128)(2,1)S(1)}, bf16[16,1,128]{2,1,0:T(2,128)(2,1)S(1)}, u32[]{:S(2)}, u32[]{:S(2)}) collective-permute-start(bf16[16,1,128]{2,1,0:T(2,128)(2,1)S(1)} %get-tuple-element.66), channel_id=1, source_target_pairs={{8,0},{16,8},{24,16},{0,24},{9,1},{17,9},{25,17},{1,25},{10,2},{18... | collective-permute-start | bytes 12296 | tf_op jit(solution)/shard_map/ppermute | solution.py:19
  65.5 3.6 %collective-permute-start.4 = (bf16[16,1,128]{2,1,0:T(2,128)(2,1)S(1)}, bf16[16,1,128]{2,1,0:T(2,128)(2,1)S(1)}, u32[]{:S(2)}, u32[]{:S(2)}) collective-permute-start(bf16[16,1,128]{2,1,0:T(2,128)(2,1)S(1)} %get-tuple-element.65), channel_id=1, source_target_pairs={{0,8},{8,16},{16,24},{24,0},{1,9},{9,17},{17,25},{25,1},{2,10},{10... | collective-permute-start | bytes 12296 | tf_op jit(solution)/shard_map/ppermute | solution.py:18
  69.1 0.8 copy-start.6
  71.5 1.0 copy-start.2
  75.6 1.8 copy-start
  76.0 0.8 copy-start.7
  80.0 10.1 %all-to-all-start.2 = ((f32[4,128,128]{2,1,0:T(8,128)}), f32[4,128,128]{2,1,0:T(8,128)S(1)}, u32[]{:S(2)}, u32[]{:S(2)}) async-start(f32[4,128,128]{2,1,0:T(8,128)} %bitcast.36), calls=%async_computation.2 | async-start | bytes 524288 | tf_op jit(solution)/shard_map/all_to_all | solution.py:159
  83.4 130.3 %reduce-scatter.2.cloned.1.call-start = ((), (), s32[]{:S(2)}) async-start(), calls=%async_computation.4 | async-start | bytes 294912 | tf_op jit(solution)/shard_map/reduce_scatter | solution.py:161
  210.9 2.0 copy-start.8
Sparse Core Ops, SparseCore 0:
  77.0 133.8 all-reduce.7
Sparse Core Ops, SparseCore 1:
  91.8 62.9 reduce-scatter.1
where the time goes:
time: 222 us; the launch traced here: 221 us
  waiting for transfers between devices  127 us (57%)
  local copies, waits for them, and re-layouts  28.2 us (13%)
  matrix products  23.8 us (11%)
  starting transfers between devices  17.2 us (8%)
  between operations  16 us (7%)
  other arithmetic  8.87 us (4%)
    psum x1, waiting for transfers between devices, per_device(): lax.psum((first_term, second_term), ('lon', 'frame'))  119 us
    dot_general x1, local copies, waits for them, and re-layouts, block_step(): jnp.einsum('tir,tih->trh', row_hot, placed_cols, preferred_element_type=j...  7.86 us
    all_to_all x1, waiting for transfers between devices, per_device(): lax.all_to_all(slot_grads, 'lon', split_axis=0, concat_axis=0, tiled=True)  6.61 us
    dot_general x18, matrix products, weight_terms(): lax.dot_general(window, flat_grad, (((0,), (0,)), ((), ())), preferred_el...  6.16 us
    dot_general x1, matrix products, block_step(): jnp.einsum('tir,tih->trh', row_hot, placed_cols, preferred_element_type=j...  5.92 us
    dot_general x9, matrix products, conv_cells(): jnp.einsum('rci,io->rco', window, weight[row_tap, col_tap], preferred_ele...  4.72 us
  transfers between devices with their start and end apart: 11, of which 4 were waited for; matrix products, arithmetic and copies ran while one was open for 9% of the time, Pallas kernels for 0%

commit v1 on v0

v1 whole, which is shorter than its diff:
```python
import functools
import math

import jax
import jax.numpy as jnp
from jax import lax
from jax.experimental import pallas as pl
from jax.experimental.pallas import tpu as pltpu
from jax.sharding import PartitionSpec as P

WIN = 7
WIDE = 144
EXT = 160
BF = jnp.bfloat16
F32 = jnp.float32
MESH = pl.DeviceIdType.MESH


def dot(a, b):
    return jnp.dot(a, b, preferred_element_type=F32)


def kernel(
    dims,
    x_ref, h_ref, w_ref, q_ref, cot_ref, rows_ref, cols_ref, own_ref,
    query_out, first_out, second_out,
    hext, xext, gext, xh, xx, xg, feat, wb, fgrad, gt, spread,
    cm, pt, qall, cmall,
    pay_send, pay_recv, halo_send, halo_recv, edge_send, edge_recv,
    ret_send, ret_recv, retall, qg_send, qg_own, qg_recv,
    grads, w1_send, w1_recv, acc, w2_own, w2_send, w2_recv, ag1, ag2, wide_out,
    pay_s, pay_r, halo_s, halo_r, edge_s, edge_r, ret_s, ret_r, qg_s, qg_r,
    w1_s, w1_r, w2_s, w2_r, a1_s, a1_r, a2_s, a2_r,
):
    lon_n, frame_n, rows_n, cols_n, chans, tracks, cap, chunk, scale = dims
    lon, frame = lax.axis_index("lon"), lax.axis_index("frame")
    slots = lon_n * cap
    half = rows_n // 2

    def lon_id(steps):
        return lax.rem(lon + steps + lon_n, lon_n)

    def frame_id(steps):
        return lax.rem(frame + steps + frame_n, frame_n)

    def remote(src, dst, send, recv, where):
        return pltpu.make_async_remote_copy(
            src_ref=src, dst_ref=dst, send_sem=send, recv_sem=recv,
            device_id=where, device_id_type=MESH,
        )

    barrier = pltpu.get_barrier_semaphore()
    for step in range(1, lon_n):
        pl.semaphore_signal(barrier, inc=1, device_id={"lon": lon_id(step)}, device_id_type=MESH)
    for step in range(1, frame_n):
        pl.semaphore_signal(barrier, inc=1, device_id={"frame": frame_id(step)}, device_id_type=MESH)

    halo_send[...] = jnp.zeros_like(halo_send)
    halo_send[0, :, 0:4] = h_ref[:, cols_n - 8 :].astype(F32)[:, 4:8].astype(BF)
    halo_send[0, :, 4:5] = x_ref[:, cols_n - 8 :].astype(F32)[:, 7:8].astype(BF)
    halo_send[1, :, 0:4] = h_ref[:, 0:8].astype(F32)[:, 0:4].astype(BF)
    halo_send[1, :, 4:5] = x_ref[:, 0:8].astype(F32)[:, 0:1].astype(BF)

    owners = own_ref[...]
    marks = (owners == lax.broadcasted_iota(jnp.int32, (16, tracks), 0)).astype(F32)
    earlier = (
        lax.broadcasted_iota(jnp.int32, (tracks, tracks), 0)
        < lax.broadcasted_iota(jnp.int32, (tracks, tracks), 1)
    ).astype(F32).astype(BF)
    before = dot(marks.astype(BF), earlier)
    rank = jnp.sum(before * marks, axis=0, keepdims=True).astype(jnp.int32)
    slot = owners * cap + rank
    cm[...] = jnp.zeros_like(cm)
    for i in range(WIN):
        cm[8 * i : 8 * i + WIN, :] = cot_ref[WIN * i : WIN * i + WIN, :].astype(F32)
    cm[56:57, :] = rows_ref[...].astype(F32)
    cm[57:58, :] = (cols_ref[...] + 3).astype(F32)
    cm_half = cm[...].astype(BF)

    pl.semaphore_wait(barrier, lon_n - 1 + frame_n - 1)
    halos = [
        remote(halo_send.at[0], halo_recv.at[0], halo_s.at[0], halo_r.at[0], {"lon": lon_id(1)}),
        remote(halo_send.at[1], halo_recv.at[1], halo_s.at[1], halo_r.at[1], {"lon": lon_id(-1)}),
    ]
    for copy in halos:
        copy.start()
    pays = []
    for step in list(range(1, lon_n)) + [0]:
        local = slot - lon_id(step) * cap
        hot = (local == lax.broadcasted_iota(jnp.int32, (cap, tracks), 0)).astype(F32).astype(BF)
        pt[step * cap : (step + 1) * cap, :] = hot
        q_part = dot(hot, q_ref[...]).astype(BF)
        c_part = lax.dot_general(
            cm_half, hot, (((1,), (1,)), ((), ())), preferred_element_type=F32
        )
        if step:
            pay_send[step - 1, 0:cap, :] = q_part
            pay_send[step - 1, cap : cap + 64, :] = c_part.astype(BF)
            copy = remote(
                pay_send.at[step - 1], pay_recv.at[step - 1], pay_s.at[step - 1],
                pay_r.at[step - 1], {"lon": lon_id(step)},
            )
            copy.start()
            pays.append(copy)
        else:
            qall[0:cap, :] = q_part
            cmall[:, 0:cap] = c_part

    for a in range(3):
        for b in range(3):
            tap = w_ref[2 - a, (2 - b) * chans : (3 - b) * chans, :].astype(F32)
            wb[a, b * chans : (b + 1) * chans, :] = tap.T.astype(BF)

    def fill(ext, src):
        ext[...] = jnp.zeros_like(ext)

        @pl.loop(0, rows_n)
        def _(r):
            ext[r + 1, 16 : 16 + cols_n, :] = src[r].astype(F32)

    def side_by_side(ext, out):
        @pl.loop(0, rows_n + 2)
        def _(r):
            for b in range(3):
                out[r, :, b * chans : (b + 1) * chans] = ext[r, 7 + b : 7 + b + WIDE, :].astype(BF)

    fill(hext, h_ref)
    fill(xext, x_ref)
    for copy in halos:
        copy.wait()
    prior = halo_recv[0].astype(F32)
    later = halo_recv[1].astype(F32)
    hext[1 : rows_n + 1, 12:16, :] = prior[:, 0:4]
    hext[1 : rows_n + 1, 16 + cols_n : 20 + cols_n, :] = later[:, 0:4]
    xext[1 : rows_n + 1, 15:16, :] = prior[:, 4:5]
    xext[1 : rows_n + 1, 16 + cols_n : 17 + cols_n, :] = later[:, 4:5]
    side_by_side(hext, xh)

    def conv(source, weight, r0):
        total = None
        for a in range(3):
            block = source[r0 + a : r0 + a + half].reshape(half * WIDE, 3 * chans)
            term = dot(block, weight[a])
            total = term if total is None else total + term
        return total

    for g in range(2):
        feat[g * half * WIDE : (g + 1) * half * WIDE, :] = conv(xh, w_ref, g * half).astype(BF)
    side_by_side(xext, xx)

    def spread_block(step):
        lanes = slice(step * cap, (step + 1) * cap)
        rows_t = cmall[56:57, lanes].astype(jnp.int32)
        cols_t = cmall[57:58, lanes].astype(jnp.int32) + 5
        placed = []
        for r in range(rows_n):
            value = jnp.zeros((8, cap), F32)
            for i in range(WIN):
                if 0 <= r - i <= rows_n - WIN:
                    value = jnp.where(rows_t == r - i, cmall[8 * i : 8 * i + 8, lanes], value)
            placed.append(value)

        @pl.loop(0, WIDE // 16)
        def _(tile):
            offset = lax.broadcasted_iota(jnp.int32, (16, cap), 0) + tile * 16 - cols_t
            hits = [offset == j for j in range(WIN)]
            for r in range(rows_n):
                value = jnp.zeros((16, cap), F32)
                for j in range(WIN):
                    value = jnp.where(hits[j], placed[r][j : j + 1, :], value)
                start = pl.multiple_of(r * WIDE + tile * 16, 16)
                spread[pl.ds(start, 16), lanes] = value.astype(BF)

    spread_block(0)
    for step in range(1, lon_n):
        pays[step - 1].wait()
        qall[step * cap : (step + 1) * cap, :] = pay_recv[step - 1, 0:cap, :]
        cmall[:, step * cap : (step + 1) * cap] = pay_recv[step - 1, cap : cap + 64, :].astype(F32)
        spread_block(step)

    for g in range(2):
        cells = slice(g * half * WIDE, (g + 1) * half * WIDE)
        fgrad[g * half : (g + 1) * half] = dot(spread[cells, :], qall[...]).reshape(
            half, WIDE, chans
        )
    edge_send[0, :, 0:4] = fgrad[:, 7 + cols_n : 11 + cols_n, :]
    edge_send[1, :, 0:4] = fgrad[:, 5:9, :]
    edge_send[:, :, 4:8] = jnp.zeros((2, rows_n, 4, chans), F32)
    edges = [
        remote(edge_send.at[0], edge_recv.at[0], edge_s.at[0], edge_r.at[0], {"lon": lon_id(1)}),
        remote(edge_send.at[1], edge_recv.at[1], edge_s.at[1], edge_r.at[1], {"lon": lon_id(-1)}),
    ]
    for copy in edges:
        copy.start()

    slot_grads = lax.dot_general(
        feat[...], spread[...], (((0,), (0,)), ((), ())), preferred_element_type=F32
    )
    retall[:, 0:cap] = slot_grads[:, 0:cap].astype(BF)
    returns = []
    for step in range(1, lon_n):
        ret_send[step - 1] = slot_grads[:, step * cap : (step + 1) * cap].astype(BF)
        copy = remote(
            ret_send.at[step - 1], ret_recv.at[step - 1], ret_s.at[step - 1],
            ret_r.at[step - 1], {"lon": lon_id(-step)},
        )
        copy.start()
        returns.append(copy)

    gext[...] = jnp.zeros_like(gext)
    for copy in edges:
        copy.wait()
    gext[1 : rows_n + 1, 16 : 16 + cols_n, :] = fgrad[:, 8 : 8 + cols_n, :]
    gext[1 : rows_n + 1, 15:19, :] = fgrad[:, 7:11, :] + edge_recv[0, :, 0:4]
    gext[1 : rows_n + 1, 13 + cols_n : 17 + cols_n, :] = (
        fgrad[:, 5 + cols_n : 9 + cols_n, :] + edge_recv[1, :, 0:4]
    )
    side_by_side(gext, xg)

    column = lax.broadcasted_iota(jnp.int32, (half, WIDE, chans), 1)
    inside = (column >= 8) & (column < 8 + cols_n)

    def weight_terms(which, source):
        for a in range(3):
            block = source[a : a + rows_n].reshape(rows_n * WIDE, 3 * chans)
            term = dot(gt[...], block) * scale
            for b in range(3):
                tap = term[:, b * chans : (b + 1) * chans].T
                grads[which, 3 * a + b] = tap
                for d in range(lon_n):
                    part = tap[d * (chans // lon_n) : (d + 1) * (chans // lon_n), :]
                    w1_send[which, d, 3 * a + b] = part.astype(BF)
        copies = []
        for step in range(1, lon_n):
            copy = remote(
                w1_send.at[which, lon_id(step)], w1_recv.at[which, step - 1],
                w1_s.at[which, step - 1], w1_r.at[which, step - 1], {"lon": lon_id(step)},
            )
            copy.start()
            copies.append(copy)
        return copies

    def over_frames(which, copies):
        part = chans // lon_n
        total = grads[which, :, pl.ds(pl.multiple_of(lon * part, part), part), :]
        for step in range(1, lon_n):
            copies[step - 1].wait()
            total = total + w1_recv[which, step - 1].astype(F32)
        if chunk * frame_n > 9 * part:
            acc[...] = jnp.zeros_like(acc)
        acc[0 : 9 * part, :] = total.reshape(9 * part, chans)
        for f in range(frame_n):
            piece = acc[f * chunk : (f + 1) * chunk, :]
            w2_own[which, f] = piece
            w2_send[which, f] = piece.astype(BF)
        out = []
        for step in range(1, frame_n):
            copy = remote(
                w2_send.at[which, frame_id(step)], w2_recv.at[which, step - 1],
                w2_s.at[which, step - 1], w2_r.at[which, step - 1], {"frame": frame_id(step)},
            )
            copy.start()
            out.append(copy)
        return out

    def gather_frames(which, copies):
        total = w2_own[which, frame]
        for step in range(1, frame_n):
            copies[step - 1].wait()
            total = total + w2_recv[which, step - 1].astype(F32)
        ag1[which, 0] = total.astype(BF)
        out = []
        for step in range(1, frame_n):
            copy = remote(
                ag1.at[which, 0], ag1.at[which, step],
                a1_s.at[which, step - 1], a1_r.at[which, step - 1], {"frame": frame_id(step)},
            )
            copy.start()
            out.append(copy)
        return out

    def gather_lon(which, copies):
        for copy in copies:
            copy.wait()
        out = []
        for step in range(1, lon_n):
            copy = remote(
                ag1.at[which], ag2.at[which, step - 1],
                a2_s.at[which, step - 1], a2_r.at[which, step - 1], {"lon": lon_id(step)},
            )
            copy.start()
            out.append(copy)
        return out

    def finish(which, copies, out):
        part = chans // lon_n
        for step in range(lon_n):
            if step:
                copies[step - 1].wait()
            for f in range(frame_n):
                if step:
                    piece = ag2[which, step - 1, f]
                else:
                    piece = ag1[which, f]
                wide_out[frame_id(-f)] = piece.astype(F32)
            for f in range(frame_n):
                acc[f * chunk : (f + 1) * chunk, :] = wide_out[f]
            out[lon_id(-step)] = acc[0 : 9 * part, :].reshape(9, part, chans).astype(BF)

    for g in range(2):
        block = gext[1 + g * half : 1 + (g + 1) * half, 8 : 8 + WIDE, :]
        block = jnp.where(inside, block, 0.0).reshape(half * WIDE, chans)
        gt[:, g * half * WIDE : (g + 1) * half * WIDE] = block.T.astype(BF)
    second1 = weight_terms(0, xh)

    for g in range(2):
        back = conv(xg, wb, g * half).reshape(half, WIDE, chans)
        active = hext[1 + g * half : 1 + (g + 1) * half, 8 : 8 + WIDE, :] > 0
        block = jnp.where(active & inside, back, 0.0).reshape(half * WIDE, chans)
        gt[:, g * half * WIDE : (g + 1) * half * WIDE] = block.T.astype(BF)
    first1 = weight_terms(1, xx)
    second2 = over_frames(0, second1)

    for step in range(1, lon_n):
        returns[step - 1].wait()
        retall[:, step * cap : (step + 1) * cap] = ret_recv[step - 1]
    home = dot(retall[...], pt[...]).T
    share = tracks // frame_n
    for f in range(frame_n):
        piece = home[f * share : (f + 1) * share, :]
        qg_own[f] = piece
        qg_send[f] = piece.astype(BF)
    qgs = []
    for step in range(1, frame_n):
        copy = remote(
            qg_send.at[frame_id(step)], qg_recv.at[step - 1], qg_s.at[step - 1],
            qg_r.at[step - 1], {"frame": frame_id(step)},
        )
        copy.start()
        qgs.append(copy)

    first2 = over_frames(1, first1)
    second3 = gather_frames(0, second2)
    first3 = gather_frames(1, first2)
    second4 = gather_lon(0, second3)
    total = qg_own[frame]
    for step in range(1, frame_n):
        qgs[step - 1].wait()
        total = total + qg_recv[step - 1].astype(F32)
    query_out[...] = total
    first4 = gather_lon(1, first3)
    finish(0, second4, second_out)
    finish(1, first4, first_out)


def per_device(
    layer_input, hidden_saved, conv_weight, queries, corr_cotangent,
    window_rows, window_cols, owner_strip,
):
    lon_n, frame_n = lax.axis_size("lon"), lax.axis_size("frame")
    _, rows_n, cols_n, chans = hidden_saved.shape
    tracks = queries.shape[0]
    cap = tracks // 4
    slots = lon_n * cap
    part = chans // lon_n
    chunk = -(-9 * part // frame_n)
    scale = 1.0 / math.sqrt(rows_n * cols_n * lon_n * frame_n)
    dims = (lon_n, frame_n, rows_n, cols_n, chans, tracks, cap, chunk, scale)
    share = tracks // frame_n
    vm = pltpu.VMEM
    dma = pltpu.SemaphoreType.DMA
    scratch = [
        vm((rows_n + 2, EXT, chans), F32),
        vm((rows_n + 2, EXT, chans), F32),
        vm((rows_n + 2, EXT, chans), F32),
        vm((rows_n + 2, WIDE, 3 * chans), BF),
        vm((rows_n + 2, WIDE, 3 * chans), BF),
        vm((rows_n + 2, WIDE, 3 * chans), BF),
        vm((rows_n * WIDE, chans), BF),
        vm((3, 3 * chans, chans), BF),
        vm((rows_n, WIDE, chans), F32),
        vm((chans, rows_n * WIDE), BF),
        vm((rows_n * WIDE, slots), BF),
        vm((64, tracks), F32),
        vm((slots, tracks), BF),
        vm((slots, chans), BF),
        vm((64, slots), F32),
        vm((lon_n - 1, cap + 64, chans), BF),
        vm((lon_n - 1, cap + 64, chans), BF),
        vm((2, rows_n, 8, chans), BF),
        vm((2, rows_n, 8, chans), BF),
        vm((2, rows_n, 8, chans), F32),
        vm((2, rows_n, 8, chans), F32),
        vm((lon_n - 1, chans, cap), BF),
        vm((lon_n - 1, chans, cap), BF),
        vm((chans, slots), BF),
        vm((frame_n, share, chans), BF),
        vm((frame_n, share, chans), F32),
        vm((frame_n - 1, share, chans), BF),
        vm((2, 9, chans, chans), F32),
        vm((2, lon_n, 9, part, chans), BF),
        vm((2, lon_n - 1, 9, part, chans), BF),
        vm((chunk * frame_n, chans), F32),
        vm((2, frame_n, chunk, chans), F32),
        vm((2, frame_n, chunk, chans), BF),
        vm((2, frame_n - 1, chunk, chans), BF),
        vm((2, frame_n, chunk, chans), BF),
        vm((2, lon_n - 1, frame_n, chunk, chans), BF),
        vm((frame_n, chunk, chans), F32),
        dma((lon_n - 1,)), dma((lon_n - 1,)),
        dma((2,)), dma((2,)),
        dma((2,)), dma((2,)),
        dma((lon_n - 1,)), dma((lon_n - 1,)),
        dma((frame_n - 1,)), dma((frame_n - 1,)),
        dma((2, lon_n - 1)), dma((2, lon_n - 1)),
        dma((2, frame_n - 1)), dma((2, frame_n - 1)),
        dma((2, frame_n - 1)), dma((2, frame_n - 1)),
        dma((2, lon_n - 1)), dma((2, lon_n - 1)),
    ]
    spec = pl.BlockSpec(memory_space=pltpu.VMEM)
    query_grad, first, second = pl.pallas_call(
        functools.partial(kernel, dims),
        out_shape=(
            jax.ShapeDtypeStruct((share, chans), F32),
            jax.ShapeDtypeStruct((lon_n, 9, part, chans), BF),
            jax.ShapeDtypeStruct((lon_n, 9, part, chans), BF),
        ),
        in_specs=[spec] * 8,
        out_specs=(spec,) * 3,
        scratch_shapes=scratch,
        compiler_params=pltpu.CompilerParams(
            collective_id=0, has_side_effects=True, vmem_limit_bytes=60 * 1024 * 1024
        ),
    )(
        layer_input[0], hidden_saved[0], conv_weight.reshape(3, 3 * chans, chans), queries,
        corr_cotangent[0], window_rows, window_cols, owner_strip[:, :, 0],
    )

    def unfold(value):
        return value.transpose(1, 0, 2, 3).reshape(3, 3, chans, chans).astype(F32)

    return query_grad, unfold(first), unfold(second)


def solution(mesh):
    placed = (
        P("frame", None, "lon", None),
        P("frame", None, "lon", None),
        P(),
        P("lon", None),
        P("frame", None, "lon"),
        P("frame", "lon"),
        P("frame", "lon"),
        P("frame", "lon", None),
    )
    return jax.shard_map(
        per_device,
        mesh=mesh,
        in_specs=placed,
        out_specs=(P(("lon", "frame"), None), P(), P()),
        check_vma=False,
    )
```

time: 222 us -> 48.9 us (0.22)
  waiting for transfers between devices: 127 us -> 0 us
  Pallas kernels: 0 us -> 44.1 us
  local copies, waits for them, and re-layouts: 28.2 us -> 2.35 us
  matrix products: 23.8 us -> 0 us
  starting transfers between devices: 17.2 us -> 0 us
  between operations: 16 us -> 0.65 us
  other arithmetic: 8.87 us -> 1.19 us
    psum x1 -> x0, waiting for transfers between devices: 119 us -> none  [per_device(): lax.psum((first_term, second_term), ('lon', 'frame'))]
    pallas_call x0 -> x1, Pallas kernels: none -> 44.1 us  [per_device(): pl.pallas_call(functools.partial(kernel, dims), out_shape=(jax.ShapeDtype...]
    dot_general x39 -> x0, matrix products: 23.8 us -> none  [the longest x18 6.16 us: weight_terms(): lax.dot_general(window, flat_grad, (((0,), (0,)), ((), ())), preferred_el...]
    all_to_all x3 -> x0, starting transfers between devices: 11 us -> none  [the longest x1 4.24 us: per_device(): lax.all_to_all(send_meta, 'lon', split_axis=0, concat_axis=0, tiled=True)]
    dot_general x2 -> x0, local copies, waits for them, and re-layouts: 10.5 us -> none  [the longest x1 7.86 us: block_step(): jnp.einsum('tir,tih->trh', row_hot, placed_cols, preferred_element_type=j...]
    all_to_all x3 -> x0, waiting for transfers between devices: 6.61 us -> none  [the longest x1 6.61 us: per_device(): lax.all_to_all(slot_grads, 'lon', split_axis=0, concat_axis=0, tiled=True)]
    ppermute x6 -> x0, starting transfers between devices: 5.84 us -> none  [the longest x2 3.59 us: padded_2(): after = lax.ppermute(first, axis, down)]
    scatter x2 -> x0, local copies, waits for them, and re-layouts: 4.77 us -> none  [the longest x1 2.99 us: per_device(): jnp.zeros((slot_count, payload.shape[1]), jnp.bfloat16).at[slot_index]]
  transfers between devices with their start and end apart: 11 -> 0, of which waited for: 4 -> 0; matrix products, arithmetic and copies ran while one was open for 9% -> 0% of each run, Pallas kernels for 0% -> 0%
where the time goes in v1:
time: 48.9 us; the launch traced here: 48.3 us
  Pallas kernels  44.1 us (90%)
  local copies, waits for them, and re-layouts  2.35 us (5%)
  other arithmetic  1.19 us (2%)
  between operations  0.65 us (1%)
    pallas_call x1, Pallas kernels, per_device(): pl.pallas_call(functools.partial(kernel, dims), out_shape=(jax.ShapeDtype...  44.1 us
    convert_element_type x2, local copies, waits for them, and re-layouts, unfold(): return value.transpose(1, 0, 2, 3).reshape(3, 3, chans, chans).astype(F32)  1.73 us
    convert_element_type x1, other arithmetic, unfold(): return value.transpose(1, 0, 2, 3).reshape(3, 3, chans, chans).astype(F32)  1.19 us

profile of v1, /device:TPU:0, one launch (start us, length us, event | category | flops | bytes accessed | tf_op | source)
XLA Modules:
  0.0 48.3 jit_solution(10278073476781288606)
XLA Ops:
  0.6 44.1 %shard_map.103 = (f32[64,128]{1,0:T(8,128)}, bf16[4,9,32,128]{3,2,1,0:T(8,128)(2,1)}, bf16[4,9,32,128]{3,2,1,0:T(8,128)(2,1)}) custom-call(bf16[16,128,128]{2,1,0:T(8,128)(2,1)} %bitcast.13, bf16[16,128,128]{2,1,0:T(8,128)(2,1)} %bitcast.14, bf16[3,384,128]{2,1,0:T(8,128)(2,1)} %bitcast.15, bf16[512,128]{1,0:T(8,128)(2,1)} %q_ref.1, ...), custom_call_target="tpu_custom_call" | custom-call | tf_op jit(solution)/shard_map/pallas_call | solution.py:421
  44.8 1.2 %convert_bitcast_fusion = (f32[9,4,32,128]{3,2,0,1:T(8,128)S(1)}, f32[9,4,32,128]{3,2,0,1:T(8,128)S(1)}) fusion(bf16[4,9,32,128]{3,2,1,0:T(8,128)(2,1)} %get-tuple-element.8, bf16[4,9,32,128]{3,2,1,0:T(8,128)(2,1)} %get-tuple-element.7), kind=kLoop, calls=%fused_computation | loop fusion | flops 294912 | bytes 1769472 | tf_op jit(solution)/shard_map/convert_element_type | solution.py:440
  46.0 0.9 %copy.12 = f32[9,4,32,128]{3,2,1,0:T(8,128)} copy(f32[9,4,32,128]{3,2,0,1:T(8,128)S(1)} %get-tuple-element.9) | data formatting | bytes 1179648 | tf_op jit(solution)/shard_map/convert_element_type | solution.py:440
  46.9 0.0 copy-start
  46.9 0.9 %copy.11 = f32[9,4,32,128]{3,2,1,0:T(8,128)} copy(f32[9,4,32,128]{3,2,0,1:T(8,128)S(1)} %get-tuple-element.10) | data formatting | bytes 1179648 | tf_op jit(solution)/shard_map/convert_element_type | solution.py:440
  47.7 0.0 copy-done
  47.7 0.6 %copy.14 = f32[64,128]{1,0:T(8,128)} copy(f32[64,128]{1,0:T(8,128)S(1)} %copy-done) | data formatting | bytes 65536
Async XLA Ops:
  46.9 0.9 %copy-start = (f32[64,128]{1,0:T(8,128)S(1)}, f32[64,128]{1,0:T(8,128)}, u32[]{:S(2)}) copy-start(f32[64,128]{1,0:T(8,128)} %get-tuple-element.14) | copy-start | bytes 98308

commit v2 on v1

--- a/solution.py
+++ b/solution.py
@@ -22,20 +22,20 @@
 
 def kernel(
     dims,
-    x_ref, h_ref, w_ref, q_ref, cot_ref, rows_ref, cols_ref, own_ref,
+    x_any, h_any, w_any, q_any, cot_ref, rows_ref, cols_ref, own_ref,
     query_out, first_out, second_out,
-    hext, xext, gext, xh, xx, xg, feat, wb, fgrad, gt, spread,
+    x_ref, h_ref, w_ref, q_ref, hext, xext, gext, xh, xx, xg, feat, wb, fgrad, gt, spread,
     cm, pt, qall, cmall,
     pay_send, pay_recv, halo_send, halo_recv, edge_send, edge_recv,
     ret_send, ret_recv, retall, qg_send, qg_own, qg_recv,
     grads, w1_send, w1_recv, acc, w2_own, w2_send, w2_recv, ag1, ag2, wide_out,
     pay_s, pay_r, halo_s, halo_r, edge_s, edge_r, ret_s, ret_r, qg_s, qg_r,
-    w1_s, w1_r, w2_s, w2_r, a1_s, a1_r, a2_s, a2_r,
+    w1_s, w1_r, w2_s, w2_r, a1_s, a1_r, a2_s, a2_r, load_s,
 ):
     lon_n, frame_n, rows_n, cols_n, chans, tracks, cap, chunk, scale = dims
     lon, frame = lax.axis_index("lon"), lax.axis_index("frame")
-    slots = lon_n * cap
     half = rows_n // 2
+    order = sorted(range(frame_n), key=lambda f: min(f, frame_n - f))
 
     def lon_id(steps):
         return lax.rem(lon + steps + lon_n, lon_n)
@@ -55,11 +55,14 @@
     for step in range(1, frame_n):
         pl.semaphore_signal(barrier, inc=1, device_id={"frame": frame_id(step)}, device_id_type=MESH)
 
-    halo_send[...] = jnp.zeros_like(halo_send)
-    halo_send[0, :, 0:4] = h_ref[:, cols_n - 8 :].astype(F32)[:, 4:8].astype(BF)
-    halo_send[0, :, 4:5] = x_ref[:, cols_n - 8 :].astype(F32)[:, 7:8].astype(BF)
-    halo_send[1, :, 0:4] = h_ref[:, 0:8].astype(F32)[:, 0:4].astype(BF)
-    halo_send[1, :, 4:5] = x_ref[:, 0:8].astype(F32)[:, 0:1].astype(BF)
+    loads = [
+        pltpu.make_async_copy(source, target, load_s.at[i])
+        for i, (source, target) in enumerate(
+            ((q_any, q_ref), (h_any, h_ref), (x_any, x_ref), (w_any, w_ref))
+        )
+    ]
+    for copy in loads:
+        copy.start()
 
     owners = own_ref[...]
     marks = (owners == lax.broadcasted_iota(jnp.int32, (16, tracks), 0)).astype(F32)
@@ -77,15 +80,8 @@
     cm[57:58, :] = (cols_ref[...] + 3).astype(F32)
     cm_half = cm[...].astype(BF)
 
-    pl.semaphore_wait(barrier, lon_n - 1 + frame_n - 1)
-    halos = [
-        remote(halo_send.at[0], halo_recv.at[0], halo_s.at[0], halo_r.at[0], {"lon": lon_id(1)}),
-        remote(halo_send.at[1], halo_recv.at[1], halo_s.at[1], halo_r.at[1], {"lon": lon_id(-1)}),
-    ]
-    for copy in halos:
-        copy.start()
-    pays = []
-    for step in list(range(1, lon_n)) + [0]:
+    loads[0].wait()
+    for step in range(lon_n):
         local = slot - lon_id(step) * cap
         hot = (local == lax.broadcasted_iota(jnp.int32, (cap, tracks), 0)).astype(F32).astype(BF)
         pt[step * cap : (step + 1) * cap, :] = hot
@@ -96,57 +92,23 @@
         if step:
             pay_send[step - 1, 0:cap, :] = q_part
             pay_send[step - 1, cap : cap + 64, :] = c_part.astype(BF)
-            copy = remote(
-                pay_send.at[step - 1], pay_recv.at[step - 1], pay_s.at[step - 1],
-                pay_r.at[step - 1], {"lon": lon_id(step)},
-            )
-            copy.start()
-            pays.append(copy)
         else:
             qall[0:cap, :] = q_part
             cmall[:, 0:cap] = c_part
 
+    loads[1].wait()
+    loads[2].wait()
+    halo_send[...] = jnp.zeros_like(halo_send)
+    halo_send[0, :, 0:4] = h_ref[:, cols_n - 8 :].astype(F32)[:, 4:8].astype(BF)
+    halo_send[0, :, 4:5] = x_ref[:, cols_n - 8 :].astype(F32)[:, 7:8].astype(BF)
+    halo_send[1, :, 0:4] = h_ref[:, 0:8].astype(F32)[:, 0:4].astype(BF)
+    halo_send[1, :, 4:5] = x_ref[:, 0:8].astype(F32)[:, 0:1].astype(BF)
+
+    loads[3].wait()
     for a in range(3):
         for b in range(3):
             tap = w_ref[2 - a, (2 - b) * chans : (3 - b) * chans, :].astype(F32)
             wb[a, b * chans : (b + 1) * chans, :] = tap.T.astype(BF)
-
-    def fill(ext, src):
-        ext[...] = jnp.zeros_like(ext)
-
-        @pl.loop(0, rows_n)
-        def _(r):
-            ext[r + 1, 16 : 16 + cols_n, :] = src[r].astype(F32)
-
-    def side_by_side(ext, out):
-        @pl.loop(0, rows_n + 2)
-        def _(r):
-            for b in range(3):
-                out[r, :, b * chans : (b + 1) * chans] = ext[r, 7 + b : 7 + b + WIDE, :].astype(BF)
-
-    fill(hext, h_ref)
-    fill(xext, x_ref)
-    for copy in halos:
-        copy.wait()
-    prior = halo_recv[0].astype(F32)
-    later = halo_recv[1].astype(F32)
-    hext[1 : rows_n + 1, 12:16, :] = prior[:, 0:4]
-    hext[1 : rows_n + 1, 16 + cols_n : 20 + cols_n, :] = later[:, 0:4]
-    xext[1 : rows_n + 1, 15:16, :] = prior[:, 4:5]
-    xext[1 : rows_n + 1, 16 + cols_n : 17 + cols_n, :] = later[:, 4:5]
-    side_by_side(hext, xh)
-
-    def conv(source, weight, r0):
-        total = None
-        for a in range(3):
-            block = source[r0 + a : r0 + a + half].reshape(half * WIDE, 3 * chans)
-            term = dot(block, weight[a])
-            total = term if total is None else total + term
-        return total
-
-    for g in range(2):
-        feat[g * half * WIDE : (g + 1) * half * WIDE, :] = conv(xh, w_ref, g * half).astype(BF)
-    side_by_side(xext, xx)
 
     def spread_block(step):
         lanes = slice(step * cap, (step + 1) * cap)
@@ -171,7 +133,61 @@
                 start = pl.multiple_of(r * WIDE + tile * 16, 16)
                 spread[pl.ds(start, 16), lanes] = value.astype(BF)
 
+    def fill(ext, src):
+        ext[...] = jnp.zeros_like(ext)
+
+        @pl.loop(0, rows_n)
+        def _(r):
+            ext[r + 1, 16 : 16 + cols_n, :] = src[r].astype(F32)
+
+    def side_by_side(ext, out):
+        @pl.loop(0, rows_n + 2)
+        def _(r):
+            for b in range(3):
+                out[r, :, b * chans : (b + 1) * chans] = ext[r, 7 + b : 7 + b + WIDE, :].astype(BF)
+
+    fill(hext, h_ref)
+    fill(xext, x_ref)
+
+    pl.semaphore_wait(barrier, lon_n - 1 + frame_n - 1)
+    halos = [
+        remote(halo_send.at[0], halo_recv.at[0], halo_s.at[0], halo_r.at[0], {"lon": lon_id(1)}),
+        remote(halo_send.at[1], halo_recv.at[1], halo_s.at[1], halo_r.at[1], {"lon": lon_id(-1)}),
+    ]
+    for copy in halos:
+        copy.start()
+    pays = [
+        remote(
+            pay_send.at[step - 1], pay_recv.at[step - 1], pay_s.at[step - 1],
+            pay_r.at[step - 1], {"lon": lon_id(step)},
+        )
+        for step in range(1, lon_n)
+    ]
+    for copy in pays:
+        copy.start()
     spread_block(0)
+    for copy in halos:
+        copy.wait()
+    prior = halo_recv[0].astype(F32)
+    later = halo_recv[1].astype(F32)
+    hext[1 : rows_n + 1, 12:16, :] = prior[:, 0:4]
+    hext[1 : rows_n + 1, 16 + cols_n : 20 + cols_n, :] = later[:, 0:4]
+    xext[1 : rows_n + 1, 15:16, :] = prior[:, 4:5]
+    xext[1 : rows_n + 1, 16 + cols_n : 17 + cols_n, :] = later[:, 4:5]
+    side_by_side(hext, xh)
+
+    def conv(source, weight, r0):
+        total = None
+        for a in range(3):
+            block = source[r0 + a : r0 + a + half].reshape(half * WIDE, 3 * chans)
+            term = dot(block, weight[a])
+            total = term if total is None else total + term
+        return total
+
+    for g in range(2):
+        feat[g * half * WIDE : (g + 1) * half * WIDE, :] = conv(xh, w_ref, g * half).astype(BF)
+    side_by_side(xext, xx)
+
     for step in range(1, lon_n):
         pays[step - 1].wait()
         qall[step * cap : (step + 1) * cap, :] = pay_recv[step - 1, 0:cap, :]
@@ -221,6 +237,7 @@
     inside = (column >= 8) & (column < 8 + cols_n)
 
     def weight_terms(which, source):
+        copies = []
         for a in range(3):
             block = source[a : a + rows_n].reshape(rows_n * WIDE, 3 * chans)
             term = dot(gt[...], block) * scale
@@ -230,21 +247,23 @@
                 for d in range(lon_n):
                     part = tap[d * (chans // lon_n) : (d + 1) * (chans // lon_n), :]
                     w1_send[which, d, 3 * a + b] = part.astype(BF)
-        copies = []
-        for step in range(1, lon_n):
-            copy = remote(
-                w1_send.at[which, lon_id(step)], w1_recv.at[which, step - 1],
-                w1_s.at[which, step - 1], w1_r.at[which, step - 1], {"lon": lon_id(step)},
-            )
-            copy.start()
-            copies.append(copy)
+            for step in range(1, lon_n):
+                copy = remote(
+                    w1_send.at[which, lon_id(step), pl.ds(3 * a, 3)],
+                    w1_recv.at[which, step - 1, pl.ds(3 * a, 3)],
+                    w1_s.at[which, a, step - 1], w1_r.at[which, a, step - 1],
+                    {"lon": lon_id(step)},
+                )
+                copy.start()
+                copies.append(copy)
         return copies
 
     def over_frames(which, copies):
         part = chans // lon_n
         total = grads[which, :, pl.ds(pl.multiple_of(lon * part, part), part), :]
+        for copy in copies:
+            copy.wait()
         for step in range(1, lon_n):
-            copies[step - 1].wait()
             total = total + w1_recv[which, step - 1].astype(F32)
         if chunk * frame_n > 9 * part:
             acc[...] = jnp.zeros_like(acc)
@@ -280,23 +299,25 @@
         return out
 
     def gather_lon(which, copies):
+        out = []
+        for f in order:
+            if f:
+                copies[f - 1].wait()
+            for step in range(1, lon_n):
+                copy = remote(
+                    ag1.at[which, f], ag2.at[which, step - 1, f],
+                    a2_s.at[which, step - 1, f], a2_r.at[which, step - 1, f],
+                    {"lon": lon_id(step)},
+                )
+                copy.start()
+                out.append(copy)
+        return out
+
+    def finish(which, copies, out):
+        part = chans // lon_n
         for copy in copies:
             copy.wait()
-        out = []
-        for step in range(1, lon_n):
-            copy = remote(
-                ag1.at[which], ag2.at[which, step - 1],
-                a2_s.at[which, step - 1], a2_r.at[which, step - 1], {"lon": lon_id(step)},
-            )
-            copy.start()
-            out.append(copy)
-        return out
-
-    def finish(which, copies, out):
-        part = chans // lon_n
         for step in range(lon_n):
-            if step:
-                copies[step - 1].wait()
             for f in range(frame_n):
                 if step:
                     piece = ag2[which, step - 1, f]
@@ -305,7 +326,9 @@
                 wide_out[frame_id(-f)] = piece.astype(F32)
             for f in range(frame_n):
                 acc[f * chunk : (f + 1) * chunk, :] = wide_out[f]
-            out[lon_id(-step)] = acc[0 : 9 * part, :].reshape(9, part, chans).astype(BF)
+            start = pl.multiple_of(lon_id(-step) * part, part)
+            grads[which, :, pl.ds(start, part), :] = acc[0 : 9 * part, :].reshape(9, part, chans)
+        out[...] = grads[which].astype(BF)
 
     for g in range(2):
         block = gext[1 + g * half : 1 + (g + 1) * half, 8 : 8 + WIDE, :]
@@ -370,6 +393,10 @@
     vm = pltpu.VMEM
     dma = pltpu.SemaphoreType.DMA
     scratch = [
+        vm((rows_n, cols_n, chans), BF),
+        vm((rows_n, cols_n, chans), BF),
+        vm((3, 3 * chans, chans), BF),
+        vm((tracks, chans), BF),
         vm((rows_n + 2, EXT, chans), F32),
         vm((rows_n + 2, EXT, chans), F32),
         vm((rows_n + 2, EXT, chans), F32),
@@ -412,20 +439,21 @@
         dma((2,)), dma((2,)),
         dma((lon_n - 1,)), dma((lon_n - 1,)),
         dma((frame_n - 1,)), dma((frame_n - 1,)),
-        dma((2, lon_n - 1)), dma((2, lon_n - 1)),
+        dma((2, 3, lon_n - 1)), dma((2, 3, lon_n - 1)),
         dma((2, frame_n - 1)), dma((2, frame_n - 1)),
         dma((2, frame_n - 1)), dma((2, frame_n - 1)),
-        dma((2, lon_n - 1)), dma((2, lon_n - 1)),
+        dma((2, lon_n - 1, frame_n)), dma((2, lon_n - 1, frame_n)),
+        dma((4,)),
     ]
     spec = pl.BlockSpec(memory_space=pltpu.VMEM)
     query_grad, first, second = pl.pallas_call(
         functools.partial(kernel, dims),
         out_shape=(
             jax.ShapeDtypeStruct((share, chans), F32),
-            jax.ShapeDtypeStruct((lon_n, 9, part, chans), BF),
-            jax.ShapeDtypeStruct((lon_n, 9, part, chans), BF),
+            jax.ShapeDtypeStruct((9, chans, chans), BF),
+            jax.ShapeDtypeStruct((9, chans, chans), BF),
         ),
-        in_specs=[spec] * 8,
+        in_specs=[pl.BlockSpec(memory_space=pl.ANY)] * 4 + [spec] * 4,
         out_specs=(spec,) * 3,
         scratch_shapes=scratch,
         compiler_params=pltpu.CompilerParams(
@@ -437,7 +465,7 @@
     )
 
     def unfold(value):
-        return value.transpose(1, 0, 2, 3).reshape(3, 3, chans, chans).astype(F32)
+        return value.reshape(3, 3, chans, chans).astype(F32)
 
     return query_grad, unfold(first), unfold(second)
 

time: 48.9 us -> 49.1 us (level)
  local copies, waits for them, and re-layouts: 2.35 us -> 0.62 us
  other arithmetic: 1.19 us -> 2.73 us
  Pallas kernels: 44.1 us -> 44.9 us
    convert_element_type x2 -> x0, local copies, waits for them, and re-layouts: 1.73 us -> none  [unfold(): return value.transpose(1, 0, 2, 3).reshape(3, 3, chans, chans).astype(F32)]
    convert_element_type x1 -> x2, other arithmetic: 1.19 us -> 2.73 us  [unfold(): return value.reshape(3, 3, chans, chans).astype(F32)]
    pallas_call x1, Pallas kernels: 44.1 us -> 44.9 us  [per_device(): pl.pallas_call(functools.partial(kernel, dims), out_shape=(jax.ShapeDtype...]
where the time goes in v2:
time: 49.1 us; the launch traced here: 48.9 us
  Pallas kernels  44.9 us (91%)
  other arithmetic  2.73 us (6%)
  between operations  0.65 us (1%)
  local copies, waits for them, and re-layouts  0.62 us (1%)
    pallas_call x1, Pallas kernels, per_device(): pl.pallas_call(functools.partial(kernel, dims), out_shape=(jax.ShapeDtype...  44.9 us
    convert_element_type x2, other arithmetic, unfold(): return value.reshape(3, 3, chans, chans).astype(F32)  2.73 us

profile of v2, /device:TPU:0, one launch (start us, length us, event | category | flops | bytes accessed | tf_op | source)
XLA Modules:
  0.0 48.9 jit_solution(1617527497722325789)
XLA Ops:
  0.6 44.9 %shard_map.103 = (f32[64,128]{1,0:T(8,128)}, bf16[9,128,128]{2,1,0:T(8,128)(2,1)}, bf16[9,128,128]{2,1,0:T(8,128)(2,1)}) custom-call(bf16[16,128,128]{2,1,0:T(8,128)(2,1)} %bitcast.9, bf16[16,128,128]{2,1,0:T(8,128)(2,1)} %bitcast.10, bf16[3,384,128]{2,1,0:T(8,128)(2,1)} %bitcast.13, bf16[512,128]{1,0:T(8,128)(2,1)} %q_any.1, bf16[49,512]{1,0:T(8,128)(2,1)} %bitcast.14, ...), custom_call_target="tpu_custom_call" | custom-call | tf_op jit(solution)/shard_map/pallas_call | solution.py:449
  45.5 0.0 copy-start
  45.6 1.9 %convert.2 = f32[3,3,128,128]{3,2,1,0:T(8,128)} convert(bf16[3,3,128,128]{3,2,1,0:T(8,128)(2,1)} %bitcast.12) | non-fusion elementwise | flops 147456 | bytes 884736 | tf_op jit(solution)/shard_map/convert_element_type | solution.py:468
  47.4 0.0 copy-done
  47.4 0.0 copy-start.1
  47.4 0.9 %convert.3 = f32[3,3,128,128]{3,2,1,0:T(8,128)} convert(bf16[3,3,128,128]{3,2,1,0:T(8,128)(2,1)S(1)} %bitcast.11) | non-fusion elementwise | flops 147456 | bytes 884736 | tf_op jit(solution)/shard_map/convert_element_type | solution.py:468
  48.3 0.0 copy-done.1
  48.3 0.6 %copy.12 = f32[64,128]{1,0:T(8,128)} copy(f32[64,128]{1,0:T(8,128)S(1)} %copy-done.1) | data formatting | bytes 65536
Async XLA Ops:
  45.5 1.9 %copy-start = (bf16[9,128,128]{2,1,0:T(8,128)(2,1)S(1)}, bf16[9,128,128]{2,1,0:T(8,128)(2,1)}, u32[]{:S(2)}) copy-start(bf16[9,128,128]{2,1,0:T(8,128)(2,1)} %get-tuple-element.8) | copy-start | bytes 884740
  47.4 0.9 %copy-start.1 = (f32[64,128]{1,0:T(8,128)S(1)}, f32[64,128]{1,0:T(8,128)}, u32[]{:S(2)}) copy-start(f32[64,128]{1,0:T(8,128)} %get-tuple-element.12) | copy-start | bytes 98308

commit v3 on v2

--- a/solution.py
+++ b/solution.py
@@ -247,15 +247,13 @@
                 for d in range(lon_n):
                     part = tap[d * (chans // lon_n) : (d + 1) * (chans // lon_n), :]
                     w1_send[which, d, 3 * a + b] = part.astype(BF)
-            for step in range(1, lon_n):
-                copy = remote(
-                    w1_send.at[which, lon_id(step), pl.ds(3 * a, 3)],
-                    w1_recv.at[which, step - 1, pl.ds(3 * a, 3)],
-                    w1_s.at[which, a, step - 1], w1_r.at[which, a, step - 1],
-                    {"lon": lon_id(step)},
-                )
-                copy.start()
-                copies.append(copy)
+        for step in range(1, lon_n):
+            copy = remote(
+                w1_send.at[which, lon_id(step)], w1_recv.at[which, step - 1],
+                w1_s.at[which, 0, step - 1], w1_r.at[which, 0, step - 1], {"lon": lon_id(step)},
+            )
+            copy.start()
+            copies.append(copy)
         return copies
 
     def over_frames(which, copies):
@@ -299,18 +297,16 @@
         return out
 
     def gather_lon(which, copies):
+        for copy in copies:
+            copy.wait()
         out = []
-        for f in order:
-            if f:
-                copies[f - 1].wait()
-            for step in range(1, lon_n):
-                copy = remote(
-                    ag1.at[which, f], ag2.at[which, step - 1, f],
-                    a2_s.at[which, step - 1, f], a2_r.at[which, step - 1, f],
-                    {"lon": lon_id(step)},
-                )
-                copy.start()
-                out.append(copy)
+        for step in range(1, lon_n):
+            copy = remote(
+                ag1.at[which], ag2.at[which, step - 1],
+                a2_s.at[which, step - 1, 0], a2_r.at[which, step - 1, 0], {"lon": lon_id(step)},
+            )
+            copy.start()
+            out.append(copy)
         return out
 
     def finish(which, copies, out):
@@ -327,8 +323,7 @@
             for f in range(frame_n):
                 acc[f * chunk : (f + 1) * chunk, :] = wide_out[f]
             start = pl.multiple_of(lon_id(-step) * part, part)
-            grads[which, :, pl.ds(start, part), :] = acc[0 : 9 * part, :].reshape(9, part, chans)
-        out[...] = grads[which].astype(BF)
+            out[:, pl.ds(start, part), :] = acc[0 : 9 * part, :].reshape(9, part, chans)
 
     for g in range(2):
         block = gext[1 + g * half : 1 + (g + 1) * half, 8 : 8 + WIDE, :]
@@ -450,8 +445,8 @@
         functools.partial(kernel, dims),
         out_shape=(
             jax.ShapeDtypeStruct((share, chans), F32),
-            jax.ShapeDtypeStruct((9, chans, chans), BF),
-            jax.ShapeDtypeStruct((9, chans, chans), BF),
+            jax.ShapeDtypeStruct((9, chans, chans), F32),
+            jax.ShapeDtypeStruct((9, chans, chans), F32),
         ),
         in_specs=[pl.BlockSpec(memory_space=pl.ANY)] * 4 + [spec] * 4,
         out_specs=(spec,) * 3,
@@ -465,7 +460,7 @@
     )
 
     def unfold(value):
-        return value.reshape(3, 3, chans, chans).astype(F32)
+        return value.reshape(3, 3, chans, chans)
 
     return query_grad, unfold(first), unfold(second)
 

time: 49.1 us -> 49.9 us (1.016); the launches traced: 48.9 us -> 49.2 us
  local copies, waits for them, and re-layouts: 0.62 us -> 4.17 us
  other arithmetic: 2.73 us -> 0 us
  Pallas kernels: 44.9 us -> 44.4 us
    unnamed x5, local copies, waits for them, and re-layouts: 0.62 us -> 4.17 us
    convert_element_type x2 -> x0, other arithmetic: 2.73 us -> none  [unfold(): return value.reshape(3, 3, chans, chans).astype(F32)]
    pallas_call x1, Pallas kernels: 44.9 us -> 44.4 us  [per_device(): pl.pallas_call(functools.partial(kernel, dims), out_shape=(jax.ShapeDtype...]
where the time goes in v3:
time: 49.9 us; the launch traced here: 49.2 us
  Pallas kernels  44.4 us (89%)
  local copies, waits for them, and re-layouts  4.17 us (8%)
  between operations  0.64 us (1%)
    pallas_call x1, Pallas kernels, per_device(): pl.pallas_call(functools.partial(kernel, dims), out_shape=(jax.ShapeDtype...  44.4 us
    unnamed x5, local copies, waits for them, and re-layouts  4.17 us

profile of v3, /device:TPU:0, one launch (start us, length us, event | category | flops | bytes accessed | tf_op | source)
XLA Modules:
  0.0 49.2 jit_solution(5593675045423730248)
XLA Ops:
  0.6 44.4 %shard_map.103 = (f32[64,128]{1,0:T(8,128)}, f32[9,128,128]{2,1,0:T(8,128)}, f32[9,128,128]{2,1,0:T(8,128)}) custom-call(bf16[16,128,128]{2,1,0:T(8,128)(2,1)} %bitcast.9, bf16[16,128,128]{2,1,0:T(8,128)(2,1)} %bitcast.10, bf16[3,384,128]{2,1,0:T(8,128)(2,1)} %bitcast.11, bf16[512,128]{1,0:T(8,128)(2,1)} %q_any.1, bf16[49,512]{1,0:T(8,128)(2,1)} %bitcast.12, ...), custom_call_target="tpu_custom_call" | custom-call | tf_op jit(solution)/shard_map/pallas_call | solution.py:444
  45.0 1.4 %copy.14 = f32[64,128]{1,0:T(8,128)} copy(f32[64,128]{1,0:T(8,128)} %get-tuple-element.12) | data formatting | bytes 65536
  46.4 0.0 copy-start
  46.4 2.0 %copy.15 = f32[3,3,128,128]{3,2,1,0:T(8,128)} copy(f32[3,3,128,128]{3,2,1,0:T(8,128)} %bitcast.8) | data formatting | bytes 1179648
  48.4 0.0 copy-done
  48.4 0.8 %copy.16 = f32[3,3,128,128]{3,2,1,0:T(8,128)} copy(f32[3,3,128,128]{3,2,1,0:T(8,128)S(1)} %bitcast.7) | data formatting | bytes 1179648
Async XLA Ops:
  46.4 2.0 %copy-start = (f32[9,128,128]{2,1,0:T(8,128)S(1)}, f32[9,128,128]{2,1,0:T(8,128)}, u32[]{:S(2)}) copy-start(f32[9,128,128]{2,1,0:T(8,128)} %get-tuple-element.8) | copy-start | bytes 1769476
